TPU v7x, 32 devices: a whole 2x2x4 slice. The times are simulated.
32 devices in a mesh: dp: 16 (over z, y, core), expert: 2 (over x).
Axes of the slice: x: 2, y: 2, z: 4, core: 2. Of those that a mesh axis runs over, the one named last changes fastest.
Arguments:
- tokens: bfloat16 [4096, 2048], P(('dp', 'expert')), may hold values from -6 to 6
- cotangent: bfloat16 [4096, 2048], P(('dp', 'expert')), may hold values from -6 to 6
- expert_ids: int32 [4096, 8], P(('dp', 'expert')), may hold values from 0 to 127, as said below
- route_weights: float32 [4096, 8], P(('dp', 'expert')), may hold values from 0.1 to 1
- join_groups: int32 [16], replicated, may hold values from 0 to 1
- w_gate: bfloat16 [2048, 1024], P('dp', 'expert'), may hold values from -0.125 to 0.125
- w_up: bfloat16 [2048, 1024], P('dp', 'expert'), may hold values from -0.125 to 0.125
- w_down: bfloat16 [2048, 1024], P('dp', 'expert'), may hold values from -0.1875 to 0.1875
Outputs:
- mixed: bfloat16 [4096, 2048], P(('dp', 'expert'))
- grad_gate: bfloat16 [2048, 1024], P('dp', 'expert')
- grad_up: bfloat16 [2048, 1024], P('dp', 'expert')
- grad_down: bfloat16 [2048, 1024], P('dp', 'expert')
Inputs may be any that keep to these rules, and one draw needn't show every extreme that they name: `expert_ids`: each row names 8 different experts; the rows of one device name expert 0 at most 16 times, and the rows of some device exactly 16 times.
All inputs are finite; a program needn't handle non-finite values.
Results may differ from a plain program's by a relative error of at most 0.014.
Values may be sent and summed in bfloat16 or wider, within the bound.
A program may use at most 64 MiB of HBM per device.

v0:
```python
import jax
import jax.numpy as jnp
from jax import lax
from jax.sharding import PartitionSpec as P


def per_device(tokens, cotangent, expert_ids, route_weights, join_groups, w_gate, w_up, w_down):
    highest = lax.Precision.HIGHEST
    tok_count = tokens.shape[0]
    slot_count = tok_count // 8
    slice_width = w_gate.shape[1]
    chosen_mask = expert_ids == 0
    routed = jnp.any(chosen_mask, -1)
    weight = jnp.sum(jnp.where(chosen_mask, route_weights, 0.0), -1)
    places = jnp.cumsum(routed.astype(jnp.int32)) - 1
    slot_ids = jnp.arange(slot_count, dtype=jnp.int32)
    chooser = ((places[None, :] == slot_ids[:, None]) & routed[None, :]).astype(jnp.float32)
    chooser_half = chooser.astype(jnp.bfloat16)
    picked_local = jnp.dot(chooser_half, tokens, preferred_element_type=jnp.float32).astype(
        jnp.bfloat16
    )
    picked = lax.all_gather(picked_local, "expert", axis=0, tiled=True)
    gate_acts = jnp.dot(
        picked, lax.all_gather(w_gate, "dp", axis=0, tiled=True), preferred_element_type=jnp.float32
    )
    up_acts = jnp.dot(
        picked, lax.all_gather(w_up, "dp", axis=0, tiled=True), preferred_element_type=jnp.float32
    )
    hidden = (jax.nn.silu(gate_acts) * up_acts).astype(jnp.bfloat16)
    trans_dims = (((1,), (1,)), ((), ()))
    full_down = lax.all_gather(w_down, "dp", axis=0, tiled=True)
    partial_out = lax.dot_general(hidden, full_down, trans_dims, preferred_element_type=jnp.float32)
    out_rows = lax.psum_scatter(
        partial_out.astype(jnp.bfloat16), "expert", scatter_dimension=0, tiled=True
    ).astype(jnp.float32)
    placed = lax.dot_general(
        chooser,
        out_rows,
        (((0,), (0,)), ((), ())),
        precision=highest,
        preferred_element_type=jnp.float32,
    )
    mixed = (placed * weight[:, None]).astype(jnp.bfloat16)
    scaled = cotangent.astype(jnp.float32) * weight[:, None]
    dpicked_local = jnp.dot(
        chooser, scaled, precision=highest, preferred_element_type=jnp.float32
    ).astype(jnp.bfloat16)
    dpicked = lax.all_gather(dpicked_local, "expert", axis=0, tiled=True)
    hidden_grad = jnp.dot(dpicked, full_down, preferred_element_type=jnp.float32)
    sigma_gate = jax.nn.sigmoid(gate_acts)
    dgate = (hidden_grad * up_acts * sigma_gate * (1.0 + gate_acts * (1.0 - sigma_gate))).astype(
        jnp.bfloat16
    )
    dup = (hidden_grad * gate_acts * sigma_gate).astype(jnp.bfloat16)
    group_total = lax.axis_size("dp")
    mine = jnp.arange(group_total, dtype=jnp.int32) == lax.axis_index("dp")
    active = 1.0 - jnp.sum(jnp.where(mine, join_groups, 0)).astype(jnp.float32)
    col_dims = (((0,), (0,)), ((), ()))

    def term_of(left, right):
        return active * lax.dot_general(left, right, col_dims, preferred_element_type=jnp.float32)

    summed = lax.psum_scatter(
        jnp.concatenate(
            [term_of(picked, dgate), term_of(picked, dup), term_of(dpicked, hidden)], axis=1
        ),
        "dp",
        scatter_dimension=0,
        tiled=True,
    )
    grad_gate = summed[:, :slice_width]
    grad_up = summed[:, slice_width : 2 * slice_width]
    grad_down = summed[:, 2 * slice_width :]
    return (
        mixed,
        grad_gate.astype(jnp.bfloat16),
        grad_up.astype(jnp.bfloat16),
        grad_down.astype(jnp.bfloat16),
    )


def solution(mesh):
    in_specs = (
        P(("dp", "expert"), None),
        P(("dp", "expert"), None),
        P(("dp", "expert"), None),
        P(("dp", "expert"), None),
        P(),
        P("dp", "expert"),
        P("dp", "expert"),
        P("dp", "expert"),
    )
    out_specs = (P(("dp", "expert"), None), P("dp", "expert"), P("dp", "expert"), P("dp", "expert"))
    return jax.shard_map(
        per_device, mesh=mesh, in_specs=in_specs, out_specs=out_specs, check_vma=False
    )
```

profile of v0, /device:TPU:0, one launch (start us, length us, event | category | flops | bytes accessed | tf_op | source)
XLA Modules:
  0.0 300.2 jit_solution(16604740441010829208)
XLA Ops:
  8.0 0.7 all-gather.6.cloned.1.call-update
  8.7 0.7 all-gather.8.cloned.1.call-update
  9.5 1.3 fusion.15
  11.4 0.7 select_reduce_fusion
  12.5 1.6 convolution_convert_fusion.1
  14.2 5.9 %all_gather.19 = bf16[32,2048]{1,0:T(8,128)(2,1)S(1)} all-gather(bf16[16,2048]{1,0:T(8,128)(2,1)S(1)} %convolution_convert_fusion.1), channel_id=1, replica_groups=mesh['dp'=16,'expert'=2] {'expert'}, dimensions={0}, use_global_device_ids=true | all-gather | bytes 196608 | tf_op jit(solution)/shard_map/all_gather | solution.py:48
  20.2 4.9 %all_gather.15 = bf16[32,2048]{1,0:T(8,128)(2,1)S(1)} all-gather(bf16[16,2048]{1,0:T(8,128)(2,1)S(1)} %convolution_convert_fusion.2), channel_id=1, replica_groups=mesh['dp'=16,'expert'=2] {'expert'}, dimensions={0}, use_global_device_ids=true | all-gather | bytes 196608 | tf_op jit(solution)/shard_map/all_gather | solution.py:22
  25.1 29.2 %all-gather.4.cloned.1.call-done = bf16[2048,512]{1,0:T(8,128)(2,1)} async-done(((bf16[128,512]{1,0:T(8,128)(2,1)}), bf16[2048,512]{1,0:T(8,128)(2,1)}) %all-gather.4.cloned.1.call-update) | async-done | bytes 2097168 | tf_op jit(solution)/shard_map/all_gather | solution.py:24
  54.4 2.0 fusion.19
  56.4 40.3 %all-gather.6.cloned.1.call-done = bf16[2048,512]{1,0:T(8,128)(2,1)} async-done(((bf16[128,512]{1,0:T(8,128)(2,1)}), bf16[2048,512]{1,0:T(8,128)(2,1)}) %all-gather.6.cloned.1.call-update) | async-done | bytes 2097168 | tf_op jit(solution)/shard_map/all_gather | solution.py:27
  96.7 2.0 multiply_convert_fusion.2
  98.8 40.3 %all-gather.8.cloned.1.call-done = bf16[2048,512]{1,0:T(8,128)(2,1)} async-done(((bf16[128,512]{1,0:T(8,128)(2,1)}), bf16[2048,512]{1,0:T(8,128)(2,1)}) %all-gather.8.cloned.1.call-update) | async-done | bytes 2097168 | tf_op jit(solution)/shard_map/all_gather | solution.py:31
  139.1 3.1 %convolution_convert_fusion = bf16[32,2048]{1,0:T(8,128)(2,1)} fusion(bf16[32,512]{1,0:T(8,128)(2,1)S(1)} %get-tuple-element.17, bf16[2048,512]{1,0:T(8,128)(2,1)} %all-gather.8.cloned.1.call-done), kind=kOutput, calls=%fused_computation.6 | convolution fusion | flops 67174400 | bytes 2260992 | tf_op jit(solution)/shard_map/dot_general | solution.py:32
  142.3 0.7 convolution_multiply_fusion
  143.5 0.8 convolution_multiply_fusion.1
  144.3 0.8 convolution_multiply_fusion.2
  145.1 5.4 %pad_maximum_fusion = f32[2048,1536]{0,1:T(8,128)} fusion(f32[2048,512]{0,1:T(8,128)S(1)} %convolution_multiply_fusion, f32[2048,512]{0,1:T(8,128)S(1)} %convolution_multiply_fusion.1, f32[2048,512]{0,1:T(8,128)S(1)} %convolution_multiply_fusion.2), kind=kLoop, calls=%fused_computation | loop fusion | flops 6291456 | bytes 25165824 | tf_op jit(solution)/shard_map/concatenate | solution.py:64
  150.5 1.0 reduce-scatter.3.cloned.1.call-done
  151.5 2.0 fusion
  153.5 136.7 %reduce-scatter.5.cloned.1.call-done = f32[128,1536]{0,1:T(8,128)} async-done(((f32[2048,1536]{0,1:T(8,128)}), f32[128,1536]{0,1:T(8,128)}) %reduce-scatter.5.cloned.1.call-update) | async-done | bytes 786448 | tf_op jit(solution)/shard_map/reduce_scatter | solution.py:63
  290.2 1.2 convert.6
  291.4 0.8 copy.19
  292.2 0.8 copy.18
  292.9 0.8 copy.17
  (20 shorter events, 2.0 us)
Async XLA Ops:
  7.2 12.9 %copy-start = (bf16[128,2048]{1,0:T(8,128)(2,1)S(1)}, bf16[128,2048]{1,0:T(8,128)(2,1)}, u32[]{:S(2)}) copy-start(bf16[128,2048]{1,0:T(8,128)(2,1)} %param.8) | copy-start | bytes 1572868
  7.2 47.2 %all-gather.4.cloned.1.call-start = ((), (), s32[]{:S(2)}) async-start(), calls=%async_computation.2 | async-start | bytes 2228224 | tf_op jit(solution)/shard_map/all_gather | solution.py:24
  7.9 88.8 %all-gather.6.cloned.1.call-start = ((), (), s32[]{:S(2)}) async-start(), calls=%async_computation.3 | async-start | bytes 2228224 | tf_op jit(solution)/shard_map/all_gather | solution.py:27
  8.7 130.4 %all-gather.8.cloned.1.call-start = ((), (), s32[]{:S(2)}) async-start(), calls=%async_computation.4 | async-start | bytes 2228224 | tf_op jit(solution)/shard_map/all_gather | solution.py:31
  9.4 142.1 %reduce-scatter.3.cloned.1.call-start = ((), (), s32[]{:S(2)}) async-start(), calls=%async_computation.5 | async-start | bytes 196608 | tf_op jit(solution)/shard_map/reduce_scatter | solution.py:33
  139.1 4.0 %copy-start.1 = (bf16[2048,512]{1,0:T(8,128)(2,1)S(1)}, bf16[2048,512]{1,0:T(8,128)(2,1)}, u32[]{:S(2)}) copy-start(bf16[2048,512]{1,0:T(8,128)(2,1)} %all-gather.8.cloned.1.call-done) | copy-start | bytes 6291460
  142.3 147.9 %reduce-scatter.5.cloned.1.call-start = ((), (), s32[]{:S(2)}) async-start(), calls=%async_computation.6 | async-start | bytes 13369344 | tf_op jit(solution)/shard_map/reduce_scatter | solution.py:63
Sparse Core Ops, SparseCore 0:
  10.2 44.1 all-gather.3
  56.5 40.1 all-gather.5
  98.9 40.1 all-gather.7
  142.4 9.0 reduce-scatter.2
  155.4 134.7 reduce-scatter.4
where the time goes:
time: 301 us; the launch traced here: 300 us
  waiting for transfers between devices  250 us (83%)
  between operations  14.5 us (5%)
  matrix products  13.7 us (5%)
  blocking collectives  10.8 us (4%)
  other arithmetic  8.91 us (3%)
    reduce_scatter x1, waiting for transfers between devices, per_device(): lax.psum_scatter(jnp.concatenate([term_of(picked, dgate), term_of(picked,...  137 us
    all_gather x1, waiting for transfers between devices, per_device(): full_down = lax.all_gather(w_down, 'dp', axis=0, tiled=True)  40.3 us
    all_gather x1, waiting for transfers between devices, per_device(): lax.all_gather(w_up, 'dp', axis=0, tiled=True)  40.3 us
    all_gather x1, waiting for transfers between devices, per_device(): lax.all_gather(w_gate, 'dp', axis=0, tiled=True)  29.2 us
  transfers between devices with their start and end apart: 5, of which 5 were waited for; matrix products, arithmetic and copies ran while one was open for 6% of the time, Pallas kernels for 0%

commit v1 on v0

--- a/solution.py
+++ b/solution.py
@@ -2,6 +2,27 @@
 import jax.numpy as jnp
 from jax import lax
 from jax.sharding import PartitionSpec as P
+
+
+def ring_gather(x, axis, dim):
+    peers, mine, span = (lax.axis_size(axis), lax.axis_index(axis), x.shape[dim])
+    upward = [(i, (i + 1) % peers) for i in range(peers)]
+    left = [(i, (i - 1) % peers) for i in range(peers)]
+    out = jnp.zeros((*x.shape[:dim], peers * span, *x.shape[dim + 1 :]), x.dtype)
+    out = lax.dynamic_update_slice_in_dim(out, x, mine * span, axis=dim)
+    from_left = from_right = x
+    middle = peers // 2
+    for step in range(1, middle + 1):
+        from_left = lax.ppermute(from_left, axis, upward)
+        out = lax.dynamic_update_slice_in_dim(
+            out, from_left, (mine - step) % peers * span, axis=dim
+        )
+        if step < peers - middle:
+            from_right = lax.ppermute(from_right, axis, left)
+            out = lax.dynamic_update_slice_in_dim(
+                out, from_right, (mine + step) % peers * span, axis=dim
+            )
+    return out
 
 
 def per_device(tokens, cotangent, expert_ids, route_weights, join_groups, w_gate, w_up, w_down):
@@ -20,9 +41,7 @@
         jnp.bfloat16
     )
     picked = lax.all_gather(picked_local, "expert", axis=0, tiled=True)
-    gate_acts = jnp.dot(
-        picked, lax.all_gather(w_gate, "dp", axis=0, tiled=True), preferred_element_type=jnp.float32
-    )
+    gate_acts = jnp.dot(picked, ring_gather(w_gate, "dp", 0), preferred_element_type=jnp.float32)
     up_acts = jnp.dot(
         picked, lax.all_gather(w_up, "dp", axis=0, tiled=True), preferred_element_type=jnp.float32
     )

time: 301 us -> 262 us (0.87)
  waiting for transfers between devices: 250 us -> 181 us
  starting transfers between devices: 0.19 us -> 31.6 us
    all_gather x1, waiting for transfers between devices: 40.3 us -> 0.01 us  [per_device(): lax.all_gather(w_up, 'dp', axis=0, tiled=True)]
    ppermute x0 -> x15, starting transfers between devices: none -> 31.4 us  [the longest x7 31.4 us: ring_gather(): from_right = lax.ppermute(from_right, axis, left)]
    ppermute x0 -> x15, waiting for transfers between devices: none -> 31 us  [the longest x8 20.7 us: ring_gather(): from_left = lax.ppermute(from_left, axis, upward)]
    all_gather x1 -> x0, waiting for transfers between devices: 29.2 us -> none  [per_device(): lax.all_gather(w_gate, 'dp', axis=0, tiled=True)]
    all_gather x1, waiting for transfers between devices: 40.3 us -> 11.7 us  [per_device(): full_down = lax.all_gather(w_down, 'dp', axis=0, tiled=True)]
  transfers between devices with their start and end apart: 5 -> 19, of which waited for: 5 -> 14; matrix products, arithmetic and copies ran while one was open for 6% -> 7% of each run, Pallas kernels for 0% -> 0%
where the time goes in v1:
time: 262 us
  waiting for transfers between devices  181 us (69%)
  starting transfers between devices  31.6 us (12%)
  between operations  14.7 us (6%)
  matrix products  12 us (5%)
  blocking collectives  9.86 us (4%)
  other arithmetic  8.94 us (3%)
  local copies, waits for them, and re-layouts  3.61 us (1%)
    reduce_scatter x1, waiting for transfers between devices, per_device(): lax.psum_scatter(jnp.concatenate([term_of(picked, dgate), term_of(picked,...  137 us
    ppermute x7, starting transfers between devices, ring_gather(): from_right = lax.ppermute(from_right, axis, left)  31.4 us
    ppermute x8, waiting for transfers between devices, ring_gather(): from_left = lax.ppermute(from_left, axis, upward)  20.7 us
    all_gather x1, waiting for transfers between devices, per_device(): full_down = lax.all_gather(w_down, 'dp', axis=0, tiled=True)  11.7 us
    ppermute x7, waiting for transfers between devices, ring_gather(): from_right = lax.ppermute(from_right, axis, left)  10.2 us
    concatenate x1, other arithmetic, per_device(): jnp.concatenate([term_of(picked, dgate), term_of(picked, dup), term_of(dp...  5.45 us
  transfers between devices with their start and end apart: 19, of which 14 were waited for; matrix products, arithmetic and copies ran while one was open for 7% of the time, Pallas kernels for 0%

profile of v1, /device:TPU:0, one launch (start us, length us, event | category | flops | bytes accessed | tf_op | source)
XLA Modules:
  0.0 261.5 jit_solution(13208961581520952991)
XLA Ops:
  8.7 5.5 %collective-permute-start.1 = (bf16[128,512]{1,0:T(8,128)(2,1)}, bf16[128,512]{1,0:T(8,128)(2,1)S(1)}, u32[]{:S(2)}, u32[]{:S(2)}) collective-permute-start(bf16[128,512]{1,0:T(8,128)(2,1)} %param.13), channel_id=1, source_target_pairs={{0,30},{2,0},{4,2},{6,4},{8,6},{10,8},{12,10},{14,12},{16,14},{18,... | collective-permute-start | bytes 393224 | tf_op jit(solution)/shard_map/ppermute | solution.py:21
  15.4 1.6 convolution_convert_fusion.1
  17.0 4.9 %all_gather.15 = bf16[32,2048]{1,0:T(8,128)(2,1)S(1)} all-gather(bf16[16,2048]{1,0:T(8,128)(2,1)S(1)} %convolution_convert_fusion.1), channel_id=1, replica_groups=mesh['dp'=16,'expert'=2] {'expert'}, dimensions={0}, use_global_device_ids=true | all-gather | bytes 196608 | tf_op jit(solution)/shard_map/all_gather | solution.py:67
  23.4 4.9 %all_gather.12 = bf16[32,2048]{1,0:T(8,128)(2,1)S(1)} all-gather(bf16[16,2048]{1,0:T(8,128)(2,1)S(1)} %convolution_convert_fusion.2), channel_id=1, replica_groups=mesh['dp'=16,'expert'=2] {'expert'}, dimensions={0}, use_global_device_ids=true | all-gather | bytes 196608 | tf_op jit(solution)/shard_map/all_gather | solution.py:43
  29.2 2.6 collective-permute-start.3
  31.9 2.5 collective-permute-done.3
  34.4 4.7 %collective-permute-start.5 = (bf16[128,512]{1,0:T(8,128)(2,1)S(1)}, bf16[128,512]{1,0:T(8,128)(2,1)S(1)}, u32[]{:S(2)}, u32[]{:S(2)}) collective-permute-start(bf16[128,512]{1,0:T(8,128)(2,1)S(1)} %collective-permute-done.3), channel_id=1, source_target_pairs={{0,30},{2,0},{4,2},{6,4},{8,6},{10,8},{12,10},{14,12},{16,14},{18,... | collective-permute-start | bytes 393224 | tf_op jit(solution)/shard_map/ppermute | solution.py:21
  39.1 3.5 %collective-permute-done.5 = bf16[128,512]{1,0:T(8,128)(2,1)S(1)} collective-permute-done((bf16[128,512]{1,0:T(8,128)(2,1)S(1)}, bf16[128,512]{1,0:T(8,128)(2,1)S(1)}, u32[]{:S(2)}, u32[]{:S(2)}) %collective-permute-start.5) | collective-permute-done | bytes 131104 | tf_op jit(solution)/shard_map/ppermute | solution.py:21
  42.6 4.7 %collective-permute-start.7 = (bf16[128,512]{1,0:T(8,128)(2,1)S(1)}, bf16[128,512]{1,0:T(8,128)(2,1)S(1)}, u32[]{:S(2)}, u32[]{:S(2)}) collective-permute-start(bf16[128,512]{1,0:T(8,128)(2,1)S(1)} %collective-permute-done.5), channel_id=1, source_target_pairs={{0,30},{2,0},{4,2},{6,4},{8,6},{10,8},{12,10},{14,12},{16,14},{18,... | collective-permute-start | bytes 393224 | tf_op jit(solution)/shard_map/ppermute | solution.py:21
  48.3 2.6 %collective-permute-done.7 = bf16[128,512]{1,0:T(8,128)(2,1)S(1)} collective-permute-done((bf16[128,512]{1,0:T(8,128)(2,1)S(1)}, bf16[128,512]{1,0:T(8,128)(2,1)S(1)}, u32[]{:S(2)}, u32[]{:S(2)}) %collective-permute-start.7) | collective-permute-done | bytes 131104 | tf_op jit(solution)/shard_map/ppermute | solution.py:21
  50.9 4.6 %collective-permute-start.9 = (bf16[128,512]{1,0:T(8,128)(2,1)S(1)}, bf16[128,512]{1,0:T(8,128)(2,1)S(1)}, u32[]{:S(2)}, u32[]{:S(2)}) collective-permute-start(bf16[128,512]{1,0:T(8,128)(2,1)S(1)} %collective-permute-done.7), channel_id=1, source_target_pairs={{0,30},{2,0},{4,2},{6,4},{8,6},{10,8},{12,10},{14,12},{16,14},{18,... | collective-permute-start | bytes 393224 | tf_op jit(solution)/shard_map/ppermute | solution.py:21
  55.5 1.7 collective-permute-done.6
  58.1 4.7 %collective-permute-start.11 = (bf16[128,512]{1,0:T(8,128)(2,1)S(1)}, bf16[128,512]{1,0:T(8,128)(2,1)S(1)}, u32[]{:S(2)}, u32[]{:S(2)}) collective-permute-start(bf16[128,512]{1,0:T(8,128)(2,1)S(1)} %collective-permute-done.9), channel_id=1, source_target_pairs={{0,30},{2,0},{4,2},{6,4},{8,6},{10,8},{12,10},{14,12},{16,14},{18,... | collective-permute-start | bytes 393224 | tf_op jit(solution)/shard_map/ppermute | solution.py:21
  62.7 1.7 collective-permute-done.8
  65.2 4.7 %collective-permute-start.13 = (bf16[128,512]{1,0:T(8,128)(2,1)S(1)}, bf16[128,512]{1,0:T(8,128)(2,1)S(1)}, u32[]{:S(2)}, u32[]{:S(2)}) collective-permute-start(bf16[128,512]{1,0:T(8,128)(2,1)S(1)} %collective-permute-done.11), channel_id=1, source_target_pairs={{0,30},{2,0},{4,2},{6,4},{8,6},{10,8},{12,10},{14,12},{16,14},{18,... | collective-permute-start | bytes 393224 | tf_op jit(solution)/shard_map/ppermute | solution.py:21
  69.9 1.7 collective-permute-done.10
  71.7 7.6 %collective-permute-done.12 = bf16[128,512]{1,0:T(8,128)(2,1)S(1)} collective-permute-done((bf16[128,512]{1,0:T(8,128)(2,1)S(1)}, bf16[128,512]{1,0:T(8,128)(2,1)S(1)}, u32[]{:S(2)}, u32[]{:S(2)}) %collective-permute-start.12) | collective-permute-done | bytes 131104 | tf_op jit(solution)/shard_map/ppermute | solution.py:16
  79.3 7.1 %collective-permute-done.14 = bf16[128,512]{1,0:T(8,128)(2,1)S(1)} collective-permute-done((bf16[128,512]{1,0:T(8,128)(2,1)S(1)}, bf16[128,512]{1,0:T(8,128)(2,1)S(1)}, u32[]{:S(2)}, u32[]{:S(2)}) %collective-permute-start.14) | collective-permute-done | bytes 131104 | tf_op jit(solution)/shard_map/ppermute | solution.py:16
  86.9 2.1 multiply_convert_fusion.2
  88.9 11.7 %all-gather.5.cloned.1.call-done = bf16[2048,512]{1,0:T(8,128)(2,1)} async-done(((bf16[128,512]{1,0:T(8,128)(2,1)}), bf16[2048,512]{1,0:T(8,128)(2,1)}) %all-gather.5.cloned.1.call-update) | async-done | bytes 2097168 | tf_op jit(solution)/shard_map/all_gather | solution.py:50
  100.6 3.0 %convolution_convert_fusion = bf16[32,2048]{1,0:T(8,128)(2,1)} fusion(bf16[32,512]{1,0:T(8,128)(2,1)S(1)} %get-tuple-element.17, bf16[2048,512]{1,0:T(8,128)(2,1)} %all-gather.5.cloned.1.call-done), kind=kOutput, calls=%fused_computation.6 | convolution fusion | flops 67174400 | bytes 2260992 | tf_op jit(solution)/shard_map/dot_general | solution.py:51
  107.2 5.4 %pad_maximum_fusion = f32[2048,1536]{0,1:T(8,128)} fusion(f32[2048,512]{0,1:T(8,128)S(1)} %convolution_multiply_fusion, f32[2048,512]{0,1:T(8,128)S(1)} %convolution_multiply_fusion.1, f32[2048,512]{0,1:T(8,128)S(1)} %convolution_multiply_fusion.2), kind=kLoop, calls=%fused_computation | loop fusion | flops 6291456 | bytes 25165824 | tf_op jit(solution)/shard_map/concatenate | solution.py:83
  112.8 2.0 fusion
  114.8 136.7 %reduce-scatter.5.cloned.1.call-done = f32[128,1536]{0,1:T(8,128)} async-done(((f32[2048,1536]{0,1:T(8,128)}), f32[128,1536]{0,1:T(8,128)}) %reduce-scatter.5.cloned.1.call-update) | async-done | bytes 786448 | tf_op jit(solution)/shard_map/reduce_scatter | solution.py:82
  (66 shorter events, 14.8 us)
Async XLA Ops:
  7.2 16.1 %copy-start = (bf16[128,2048]{1,0:T(8,128)(2,1)S(1)}, bf16[128,2048]{1,0:T(8,128)(2,1)}, u32[]{:S(2)}) copy-start(bf16[128,2048]{1,0:T(8,128)(2,1)} %param.8) | copy-start | bytes 1572868
  7.2 79.7 %all-gather.3.cloned.1.call-start = ((), (), s32[]{:S(2)}) async-start(), calls=%async_computation.2 | async-start | bytes 2228224 | tf_op jit(solution)/shard_map/all_gather | solution.py:46
  7.9 92.7 %all-gather.5.cloned.1.call-start = ((), (), s32[]{:S(2)}) async-start(), calls=%async_computation.3 | async-start | bytes 2228224 | tf_op jit(solution)/shard_map/all_gather | solution.py:50
  8.7 104.1 %reduce-scatter.3.cloned.1.call-start = ((), (), s32[]{:S(2)}) async-start(), calls=%async_computation.4 | async-start | bytes 196608 | tf_op jit(solution)/shard_map/reduce_scatter | solution.py:52
  8.7 20.5 %collective-permute-start.1 = (bf16[128,512]{1,0:T(8,128)(2,1)}, bf16[128,512]{1,0:T(8,128)(2,1)S(1)}, u32[]{:S(2)}, u32[]{:S(2)}) collective-permute-start(bf16[128,512]{1,0:T(8,128)(2,1)} %param.13), channel_id=1, source_target_pairs={{0,30},{2,0},{4,2},{6,4},{8,6},{10,8},{12,10},{14,12},{16,14},{18,... | collective-permute-start | bytes 393224 | tf_op jit(solution)/shard_map/ppermute | solution.py:21
  14.2 17.6 %collective-permute-start = (bf16[128,512]{1,0:T(8,128)(2,1)}, bf16[128,512]{1,0:T(8,128)(2,1)S(1)}, u32[]{:S(2)}, u32[]{:S(2)}) collective-permute-start(bf16[128,512]{1,0:T(8,128)(2,1)} %param.13), channel_id=1, source_target_pairs={{0,2},{2,4},{4,6},{6,8},{8,10},{10,12},{12,14},{14,16},{16,18},{18... | collective-permute-start | bytes 393224 | tf_op jit(solution)/shard_map/ppermute | solution.py:16
  15.3 13.9 %copy-start.2 = (bf16[128,512]{1,0:T(8,128)(2,1)S(1)}, bf16[128,512]{1,0:T(8,128)(2,1)}, u32[]{:S(2)}) copy-start(bf16[128,512]{1,0:T(8,128)(2,1)} %param.13) | copy-start | bytes 393220
  29.2 5.1 %collective-permute-start.3 = (bf16[128,512]{1,0:T(8,128)(2,1)S(1)}, bf16[128,512]{1,0:T(8,128)(2,1)S(1)}, u32[]{:S(2)}, u32[]{:S(2)}) collective-permute-start(bf16[128,512]{1,0:T(8,128)(2,1)S(1)} %collective-permute-done.1), channel_id=1, source_target_pairs={{0,30},{2,0},{4,2},{6,4},{8,6},{10,8},{12,10},{14,12},{16,14},{18,... | collective-permute-start | bytes 393224 | tf_op jit(solution)/shard_map/ppermute | solution.py:21
  31.8 7.2 %collective-permute-start.2 = (bf16[128,512]{1,0:T(8,128)(2,1)S(1)}, bf16[128,512]{1,0:T(8,128)(2,1)S(1)}, u32[]{:S(2)}, u32[]{:S(2)}) collective-permute-start(bf16[128,512]{1,0:T(8,128)(2,1)S(1)} %collective-permute-done), channel_id=1, source_target_pairs={{0,2},{2,4},{4,6},{6,8},{8,10},{10,12},{12,14},{14,16},{16,18},{18... | collective-permute-start | bytes 393224 | tf_op jit(solution)/shard_map/ppermute | solution.py:16
  34.4 8.2 %collective-permute-start.5 = (bf16[128,512]{1,0:T(8,128)(2,1)S(1)}, bf16[128,512]{1,0:T(8,128)(2,1)S(1)}, u32[]{:S(2)}, u32[]{:S(2)}) collective-permute-start(bf16[128,512]{1,0:T(8,128)(2,1)S(1)} %collective-permute-done.3), channel_id=1, source_target_pairs={{0,30},{2,0},{4,2},{6,4},{8,6},{10,8},{12,10},{14,12},{16,14},{18,... | collective-permute-start | bytes 393224 | tf_op jit(solution)/shard_map/ppermute | solution.py:21
  39.0 9.2 %collective-permute-start.4 = (bf16[128,512]{1,0:T(8,128)(2,1)S(1)}, bf16[128,512]{1,0:T(8,128)(2,1)S(1)}, u32[]{:S(2)}, u32[]{:S(2)}) collective-permute-start(bf16[128,512]{1,0:T(8,128)(2,1)S(1)} %collective-permute-done.2), channel_id=1, source_target_pairs={{0,2},{2,4},{4,6},{6,8},{8,10},{10,12},{12,14},{14,16},{16,18},{18... | collective-permute-start | bytes 393224 | tf_op jit(solution)/shard_map/ppermute | solution.py:16
  42.6 8.3 %collective-permute-start.7 = (bf16[128,512]{1,0:T(8,128)(2,1)S(1)}, bf16[128,512]{1,0:T(8,128)(2,1)S(1)}, u32[]{:S(2)}, u32[]{:S(2)}) collective-permute-start(bf16[128,512]{1,0:T(8,128)(2,1)S(1)} %collective-permute-done.5), channel_id=1, source_target_pairs={{0,30},{2,0},{4,2},{6,4},{8,6},{10,8},{12,10},{14,12},{16,14},{18,... | collective-permute-start | bytes 393224 | tf_op jit(solution)/shard_map/ppermute | solution.py:21
  48.2 9.0 %collective-permute-start.6 = (bf16[128,512]{1,0:T(8,128)(2,1)S(1)}, bf16[128,512]{1,0:T(8,128)(2,1)S(1)}, u32[]{:S(2)}, u32[]{:S(2)}) collective-permute-start(bf16[128,512]{1,0:T(8,128)(2,1)S(1)} %collective-permute-done.4), channel_id=1, source_target_pairs={{0,2},{2,4},{4,6},{6,8},{8,10},{10,12},{12,14},{14,16},{16,18},{18... | collective-permute-start | bytes 393224 | tf_op jit(solution)/shard_map/ppermute | solution.py:16
  50.9 7.1 %collective-permute-start.9 = (bf16[128,512]{1,0:T(8,128)(2,1)S(1)}, bf16[128,512]{1,0:T(8,128)(2,1)S(1)}, u32[]{:S(2)}, u32[]{:S(2)}) collective-permute-start(bf16[128,512]{1,0:T(8,128)(2,1)S(1)} %collective-permute-done.7), channel_id=1, source_target_pairs={{0,30},{2,0},{4,2},{6,4},{8,6},{10,8},{12,10},{14,12},{16,14},{18,... | collective-permute-start | bytes 393224 | tf_op jit(solution)/shard_map/ppermute | solution.py:21
  57.2 7.2 %collective-permute-start.8 = (bf16[128,512]{1,0:T(8,128)(2,1)S(1)}, bf16[128,512]{1,0:T(8,128)(2,1)S(1)}, u32[]{:S(2)}, u32[]{:S(2)}) collective-permute-start(bf16[128,512]{1,0:T(8,128)(2,1)S(1)} %collective-permute-done.6), channel_id=1, source_target_pairs={{0,2},{2,4},{4,6},{6,8},{8,10},{10,12},{12,14},{14,16},{16,18},{18... | collective-permute-start | bytes 393224 | tf_op jit(solution)/shard_map/ppermute | solution.py:16
  58.1 7.2 %collective-permute-start.11 = (bf16[128,512]{1,0:T(8,128)(2,1)S(1)}, bf16[128,512]{1,0:T(8,128)(2,1)S(1)}, u32[]{:S(2)}, u32[]{:S(2)}) collective-permute-start(bf16[128,512]{1,0:T(8,128)(2,1)S(1)} %collective-permute-done.9), channel_id=1, source_target_pairs={{0,30},{2,0},{4,2},{6,4},{8,6},{10,8},{12,10},{14,12},{16,14},{18,... | collective-permute-start | bytes 393224 | tf_op jit(solution)/shard_map/ppermute | solution.py:21
  64.4 7.2 %collective-permute-start.10 = (bf16[128,512]{1,0:T(8,128)(2,1)S(1)}, bf16[128,512]{1,0:T(8,128)(2,1)S(1)}, u32[]{:S(2)}, u32[]{:S(2)}) collective-permute-start(bf16[128,512]{1,0:T(8,128)(2,1)S(1)} %collective-permute-done.8), channel_id=1, source_target_pairs={{0,2},{2,4},{4,6},{6,8},{8,10},{10,12},{12,14},{14,16},{16,18},{18... | collective-permute-start | bytes 393224 | tf_op jit(solution)/shard_map/ppermute | solution.py:16
  65.2 14.0 %collective-permute-start.13 = (bf16[128,512]{1,0:T(8,128)(2,1)S(1)}, bf16[128,512]{1,0:T(8,128)(2,1)S(1)}, u32[]{:S(2)}, u32[]{:S(2)}) collective-permute-start(bf16[128,512]{1,0:T(8,128)(2,1)S(1)} %collective-permute-done.11), channel_id=1, source_target_pairs={{0,30},{2,0},{4,2},{6,4},{8,6},{10,8},{12,10},{14,12},{16,14},{18,... | collective-permute-start | bytes 393224 | tf_op jit(solution)/shard_map/ppermute | solution.py:21
  71.7 7.6 %collective-permute-start.12 = (bf16[128,512]{1,0:T(8,128)(2,1)S(1)}, bf16[128,512]{1,0:T(8,128)(2,1)S(1)}, u32[]{:S(2)}, u32[]{:S(2)}) collective-permute-start(bf16[128,512]{1,0:T(8,128)(2,1)S(1)} %collective-permute-done.10), channel_id=1, source_target_pairs={{0,2},{2,4},{4,6},{6,8},{8,10},{10,12},{12,14},{14,16},{16,18},{18... | collective-permute-start | bytes 393224 | tf_op jit(solution)/shard_map/ppermute | solution.py:16
  79.3 7.1 %collective-permute-start.14 = (bf16[128,512]{1,0:T(8,128)(2,1)S(1)}, bf16[128,512]{1,0:T(8,128)(2,1)S(1)}, u32[]{:S(2)}, u32[]{:S(2)}) collective-permute-start(bf16[128,512]{1,0:T(8,128)(2,1)S(1)} %collective-permute-done.12), channel_id=1, source_target_pairs={{0,2},{2,4},{4,6},{6,8},{8,10},{10,12},{12,14},{14,16},{16,18},{18... | collective-permute-start | bytes 393224 | tf_op jit(solution)/shard_map/ppermute | solution.py:16
  103.6 1.6 copy-start.1
  103.6 147.9 %reduce-scatter.5.cloned.1.call-start = ((), (), s32[]{:S(2)}) async-start(), calls=%async_computation.5 | async-start | bytes 13369344 | tf_op jit(solution)/shard_map/reduce_scatter | solution.py:82
Sparse Core Ops, SparseCore 0:
  10.2 46.1 all-gather.2
  58.6 41.9 all-gather.4
  103.7 9.0 reduce-scatter.2
  116.7 134.7 reduce-scatter.4
